TPU v7x, 256 devices: a whole 4x4x8 slice. The times are simulated.
256 devices in a mesh: row: 32 (over x, z), feat: 8 (over y, core).
Axes of the slice: x: 4, y: 4, z: 8, core: 2. Of those that a mesh axis runs over, the one named last changes fastest.
Arguments:
- scores: float32 [192, 1024], P('row'), may hold values from -8 to 8, as said below
- labels: int32 [192, 1024], P('row'), may hold values from 0 to 4
- counts: int32 [192], P('row'), may hold values from 1 to 1024, 147456 in all
- bin_codes: int32 [192, 768, 1024], P('row', 'feat'), may hold values from 0 to 255
- row_child: int32 [192, 1024], P('row'), may hold values from 0 to 15
- smaller: int32 [8], replicated, may hold values from 0 to 1, as said below
- parent_hist: float32 [256, 8, 1536], P('row', None, 'feat'), may hold values from -10 to 10
Outputs:
- children: float32 [256, 8, 3072], P('row', None, 'feat')
- best_gain: float32 [8], replicated
Inputs may be any that keep to these rules, and one draw needn't show every extreme that they name: Each query's scores never rise from one slot to the next. The counts of all queries sum to 147456, and some query is full. `smaller`: exactly half of the 8 parents have the value 1.
All inputs are finite; a program needn't handle non-finite values. No bound on the sum of `counts` on one device may be relied on, other than what follows from the above.
Results may differ from a plain program's by a relative error of at most 0.0028.
Values may be sent and summed in bfloat16 or wider, within the bound.
No kernel may reach another device: no remote copies, remote signals or barrier semaphores. Data moves between devices by JAX's collectives and lax.ppermute only.
A program may use at most 64 MiB of HBM per device.

v0:
```python
import math
import jax
import jax.numpy as jnp
from jax import lax
from jax.sharding import PartitionSpec as P

levels = 5
reg_lambda = 1.0


def query_terms(labels, counts):
    slot_count = labels.shape[1]
    position = jnp.arange(slot_count, dtype=jnp.int32)
    usable = position[None, :] < counts[:, None]
    grades = jnp.arange(levels, dtype=jnp.int32)
    same_grade = labels[:, :, None] == grades[None, None, :]
    label_hot = (same_grade & usable[:, :, None]).astype(jnp.int32)
    per_grade = jnp.sum(label_hot, axis=1)
    above_count = jnp.sum(
        per_grade[:, None, :] * (grades[None, None, :] > labels[:, :, None]).astype(jnp.int32),
        axis=2,
    )
    running = jnp.cumsum(label_hot, axis=1) - label_hot
    before_count = jnp.sum(running * same_grade.astype(jnp.int32), axis=2)
    ideal_rank = above_count + before_count
    rel_gain = jnp.exp2(labels.astype(jnp.float32)) - 1.0
    discount = 1.0 / jnp.log2(position.astype(jnp.float32) + 2.0)
    ideal_terms = jnp.where(usable, rel_gain / jnp.log2(ideal_rank.astype(jnp.float32) + 2.0), 0.0)
    inv_ideal = 1.0 / jnp.maximum(jnp.sum(ideal_terms, axis=1), 1.0)
    return (usable, rel_gain, discount, inv_ideal)


def pair_block(
    row_scores,
    row_labels,
    row_gain,
    row_disc,
    row_usable,
    scores,
    labels,
    rel_gain,
    discount,
    usable,
    inv_ideal,
):
    score_gap = row_scores[:, :, None] - scores[:, None, :]
    higher = row_labels[:, :, None] > labels[:, None, :]
    live_pair = (
        (row_labels[:, :, None] != labels[:, None, :]) & row_usable[:, :, None] & usable[:, None, :]
    )
    pair_sign = jnp.where(higher, 1.0, -1.0)
    pair_prob = jax.nn.sigmoid(-pair_sign * score_gap)
    pair_weight = (
        jnp.abs(row_gain[:, :, None] - rel_gain[:, None, :])
        * jnp.abs(row_disc[None, :, None] - discount[None, None, :])
        * inv_ideal[:, None, None]
    )
    lam_grad = -jnp.sum(jnp.where(live_pair, pair_sign * pair_prob * pair_weight, 0.0), axis=2)
    lam_hess = jnp.sum(
        jnp.where(live_pair, pair_prob * (1.0 - pair_prob) * pair_weight, 0.0), axis=2
    )
    return (lam_grad, lam_hess)


def node_weights(lam_g16, lam_h16, row_child, smaller):
    parents = smaller.shape[0]
    built_node = 2 * jnp.arange(parents, dtype=jnp.int32) + smaller
    member = (row_child[:, :, None] == built_node[None, None, :]).astype(jnp.bfloat16)
    stats = jnp.stack((lam_g16, lam_h16), axis=-1)
    weights = member[:, :, :, None] * stats[:, :, None, :]
    return weights.reshape(row_child.shape[0], row_child.shape[1], parents * 2)


def split_gain(left_sums, totals):
    grad_left = left_sums[..., 0]
    hess_left = left_sums[..., 1]
    grad_total = totals[..., 0]
    hess_total = totals[..., 1]
    grad_right = grad_total - grad_left
    return (
        grad_left * grad_left / (hess_left + reg_lambda)
        + grad_right * grad_right / (hess_total - hess_left + reg_lambda)
        - grad_total * grad_total / (hess_total + reg_lambda)
    )


def bin_histogram(bin_codes, weights, number):
    feat_dev = bin_codes.shape[1]
    node_cols = weights.shape[2]
    feat_block = math.gcd(feat_dev, 4)
    bin_marks = jnp.arange(number, dtype=jnp.int32)

    def one_block(first_feat):
        code_block = lax.dynamic_slice_in_dim(bin_codes, first_feat, feat_block, 1)
        one_hot = (code_block[..., None] == bin_marks).astype(jnp.bfloat16)
        return jnp.einsum("qfnb,qnk->bfk", one_hot, weights, preferred_element_type=jnp.float32)

    pieces = lax.map(one_block, jnp.arange(feat_dev // feat_block, dtype=jnp.int32) * feat_block)
    pieces = jnp.transpose(pieces, (1, 0, 2, 3)).reshape(number, feat_dev, node_cols // 2, 2)
    return jnp.transpose(pieces, (0, 2, 1, 3)).reshape(number, node_cols // 2, feat_dev * 2)


def shards(scores, labels, counts, bin_codes, row_child, smaller, parent_hist):
    query_dev, slot_count = scores.shape
    feat_count = lax.axis_size("feat")
    row_span = slot_count // feat_count
    usable, rel_gain, discount, inv_ideal = query_terms(labels, counts)

    def block_terms(offset):

        def rows_of(array):
            return lax.dynamic_slice_in_dim(array, offset, row_span, 1)

        return pair_block(
            rows_of(scores),
            rows_of(labels),
            rows_of(rel_gain),
            lax.dynamic_slice_in_dim(discount, offset, row_span, 0),
            rows_of(usable),
            scores,
            labels,
            rel_gain,
            discount,
            usable,
            inv_ideal,
        )

    every_grad, every_hess = lax.map(
        block_terms, jnp.arange(feat_count, dtype=jnp.int32) * row_span
    )
    lam_g16 = (
        jnp.transpose(every_grad, (1, 0, 2)).reshape(query_dev, slot_count).astype(jnp.bfloat16)
    )
    lam_h16 = (
        jnp.transpose(every_hess, (1, 0, 2)).reshape(query_dev, slot_count).astype(jnp.bfloat16)
    )
    weights = node_weights(lam_g16, lam_h16, row_child, smaller)
    parents = smaller.shape[0]
    feat_dev = bin_codes.shape[1]
    bin_span = parent_hist.shape[0]
    bin_total = bin_span * lax.axis_size("row")
    all_bins = lax.psum(bin_histogram(bin_codes, weights, bin_total), "row")
    stacked_all = all_bins.reshape(bin_total, parents, feat_dev, 2)
    left_sums = jnp.cumsum(stacked_all, axis=0)
    totals = jnp.sum(stacked_all, axis=0)
    gains = split_gain(left_sums[:-1], totals[None])
    best_gain = lax.pmax(jnp.max(gains, axis=(0, 2)), "feat")
    own_bins = lax.dynamic_slice_in_dim(all_bins, lax.axis_index("row") * bin_span, bin_span, 0)
    built = own_bins.reshape(bin_span, parents, feat_dev, 2)
    sibling = parent_hist.reshape(bin_span, parents, feat_dev, 2) - built
    chosen = smaller[:, None] == jnp.arange(2, dtype=jnp.int32)[None, :]
    children = jnp.where(
        chosen[None, :, None, :, None], built[:, :, :, None, :], sibling[:, :, :, None, :]
    )
    return (children.reshape(bin_span, parents, feat_dev * 4), best_gain)


def solution(mesh):
    placed = (
        P("row", None),
        P("row", None),
        P("row"),
        P("row", "feat", None),
        P("row", None),
        P(),
        P("row", None, "feat"),
    )
    return jax.shard_map(
        shards, mesh=mesh, in_specs=placed, out_specs=(P("row", None, "feat"), P()), check_vma=False
    )
```

profile of v0, /device:TPU:1, one launch (start us, length us, event | category | flops | bytes accessed | tf_op | source)
XLA Modules:
  0.0 608.6 jit_solution(1435842050585580470)
XLA Ops:
  22.8 72.7 %while.24 = (s32[]{:T(128)}, bf16[8,6,128]{2,1,0:T(8,128)(2,1)S(1)}, bf16[8,6,128]{2,1,0:T(8,128)(2,1)S(1)}, s32[8]{0:T(128)S(1)}, s32[6,1024]{1,0:T(8,128)}, /*...) while((s32[]{:T(128)}, ...), condition=%wide.region_9.10_spmd.clone, body=%wide.region_6.9_spmd.clone.sunk | while | flops 19135748 | bytes 1181155 | solution.py:128
  95.7 302.4 %while.25 = (s32[]{:T(128)}, f32[24,256,4,16]{1,3,2,0:T(8,128)S(1)}, s32[24]{0:T(128)S(1)}, s32[6,96,1024]{2,1,0:T(8,128)}, bf16[6,1024,2]{1,2,0:T(2,128)(2,1)S(...) while((s32[]{:T(128)}, f32[24,256,4,16]{1,3,2,0:T(8,128)S(1)}, ...), condition=%wide.region_11.12_spmd.clone, body=%wide.region_10.11_spmd.clone.sunk | while | flops 207716352 | bytes 1499291 | solution.py:98
  99.6 8.6 %fusion.33 = f32[24,256,4,16]{1,3,2,0:T(8,128)S(1)} fusion(f32[24,256,4,16]{1,3,2,0:T(8,128)S(1)} %get-tuple-element.361, s32[]{:T(128)S(6)} %copy.91, bf16[6,1024,16,1]{1,2,0,3:T(8,128)(2,1)S(1)} %reshape.218, s32[6,4,1024]{2,0,1:T(8,128)S(1)} %copy.76), kind=kOutput, calls=%fused_computation.29.clone.1 | convolution fusion | flops 207618048 | bytes 393220 | tf_op jit(solution)/shard_map/while/body/eval_jaxpr/qfnb,qnk->bfk/dot_general | solution.py:96
  124.8 8.6 %fusion.33 = f32[24,256,4,16]{1,3,2,0:T(8,128)S(1)} fusion(f32[24,256,4,16]{1,3,2,0:T(8,128)S(1)} %get-tuple-element.361, s32[]{:T(128)S(6)} %copy.91, bf16[6,1024,16,1]{1,2,0,3:T(8,128)(2,1)S(1)} %reshape.218, s32[6,4,1024]{2,0,1:T(8,128)S(1)} %copy.76), kind=kOutput, calls=%fused_computation.29.clone.1 | convolution fusion | flops 207618048 | bytes 393220 | tf_op jit(solution)/shard_map/while/body/eval_jaxpr/qfnb,qnk->bfk/dot_general | solution.py:96
  150.0 8.6 %fusion.33 = f32[24,256,4,16]{1,3,2,0:T(8,128)S(1)} fusion(f32[24,256,4,16]{1,3,2,0:T(8,128)S(1)} %get-tuple-element.361, s32[]{:T(128)S(6)} %copy.91, bf16[6,1024,16,1]{1,2,0,3:T(8,128)(2,1)S(1)} %reshape.218, s32[6,4,1024]{2,0,1:T(8,128)S(1)} %copy.76), kind=kOutput, calls=%fused_computation.29.clone.1 | convolution fusion | flops 207618048 | bytes 393220 | tf_op jit(solution)/shard_map/while/body/eval_jaxpr/qfnb,qnk->bfk/dot_general | solution.py:96
  175.3 8.6 %fusion.33 = f32[24,256,4,16]{1,3,2,0:T(8,128)S(1)} fusion(f32[24,256,4,16]{1,3,2,0:T(8,128)S(1)} %get-tuple-element.361, s32[]{:T(128)S(6)} %copy.91, bf16[6,1024,16,1]{1,2,0,3:T(8,128)(2,1)S(1)} %reshape.218, s32[6,4,1024]{2,0,1:T(8,128)S(1)} %copy.76), kind=kOutput, calls=%fused_computation.29.clone.1 | convolution fusion | flops 207618048 | bytes 393220 | tf_op jit(solution)/shard_map/while/body/eval_jaxpr/qfnb,qnk->bfk/dot_general | solution.py:96
  187.9 8.6 %fusion.33 = f32[24,256,4,16]{1,3,2,0:T(8,128)S(1)} fusion(f32[24,256,4,16]{1,3,2,0:T(8,128)S(1)} %get-tuple-element.361, s32[]{:T(128)S(6)} %copy.91, bf16[6,1024,16,1]{1,2,0,3:T(8,128)(2,1)S(1)} %reshape.218, s32[6,4,1024]{2,0,1:T(8,128)S(1)} %copy.76), kind=kOutput, calls=%fused_computation.29.clone.1 | convolution fusion | flops 207618048 | bytes 393220 | tf_op jit(solution)/shard_map/while/body/eval_jaxpr/qfnb,qnk->bfk/dot_general | solution.py:96
  200.5 8.6 %fusion.33 = f32[24,256,4,16]{1,3,2,0:T(8,128)S(1)} fusion(f32[24,256,4,16]{1,3,2,0:T(8,128)S(1)} %get-tuple-element.361, s32[]{:T(128)S(6)} %copy.91, bf16[6,1024,16,1]{1,2,0,3:T(8,128)(2,1)S(1)} %reshape.218, s32[6,4,1024]{2,0,1:T(8,128)S(1)} %copy.76), kind=kOutput, calls=%fused_computation.29.clone.1 | convolution fusion | flops 207618048 | bytes 393220 | tf_op jit(solution)/shard_map/while/body/eval_jaxpr/qfnb,qnk->bfk/dot_general | solution.py:96
  213.1 8.6 %fusion.33 = f32[24,256,4,16]{1,3,2,0:T(8,128)S(1)} fusion(f32[24,256,4,16]{1,3,2,0:T(8,128)S(1)} %get-tuple-element.361, s32[]{:T(128)S(6)} %copy.91, bf16[6,1024,16,1]{1,2,0,3:T(8,128)(2,1)S(1)} %reshape.218, s32[6,4,1024]{2,0,1:T(8,128)S(1)} %copy.76), kind=kOutput, calls=%fused_computation.29.clone.1 | convolution fusion | flops 207618048 | bytes 393220 | tf_op jit(solution)/shard_map/while/body/eval_jaxpr/qfnb,qnk->bfk/dot_general | solution.py:96
  225.7 8.6 %fusion.33 = f32[24,256,4,16]{1,3,2,0:T(8,128)S(1)} fusion(f32[24,256,4,16]{1,3,2,0:T(8,128)S(1)} %get-tuple-element.361, s32[]{:T(128)S(6)} %copy.91, bf16[6,1024,16,1]{1,2,0,3:T(8,128)(2,1)S(1)} %reshape.218, s32[6,4,1024]{2,0,1:T(8,128)S(1)} %copy.76), kind=kOutput, calls=%fused_computation.29.clone.1 | convolution fusion | flops 207618048 | bytes 393220 | tf_op jit(solution)/shard_map/while/body/eval_jaxpr/qfnb,qnk->bfk/dot_general | solution.py:96
  238.3 8.6 %fusion.33 = f32[24,256,4,16]{1,3,2,0:T(8,128)S(1)} fusion(f32[24,256,4,16]{1,3,2,0:T(8,128)S(1)} %get-tuple-element.361, s32[]{:T(128)S(6)} %copy.91, bf16[6,1024,16,1]{1,2,0,3:T(8,128)(2,1)S(1)} %reshape.218, s32[6,4,1024]{2,0,1:T(8,128)S(1)} %copy.76), kind=kOutput, calls=%fused_computation.29.clone.1 | convolution fusion | flops 207618048 | bytes 393220 | tf_op jit(solution)/shard_map/while/body/eval_jaxpr/qfnb,qnk->bfk/dot_general | solution.py:96
  250.9 8.6 %fusion.33 = f32[24,256,4,16]{1,3,2,0:T(8,128)S(1)} fusion(f32[24,256,4,16]{1,3,2,0:T(8,128)S(1)} %get-tuple-element.361, s32[]{:T(128)S(6)} %copy.91, bf16[6,1024,16,1]{1,2,0,3:T(8,128)(2,1)S(1)} %reshape.218, s32[6,4,1024]{2,0,1:T(8,128)S(1)} %copy.76), kind=kOutput, calls=%fused_computation.29.clone.1 | convolution fusion | flops 207618048 | bytes 393220 | tf_op jit(solution)/shard_map/while/body/eval_jaxpr/qfnb,qnk->bfk/dot_general | solution.py:96
  263.5 8.6 %fusion.33 = f32[24,256,4,16]{1,3,2,0:T(8,128)S(1)} fusion(f32[24,256,4,16]{1,3,2,0:T(8,128)S(1)} %get-tuple-element.361, s32[]{:T(128)S(6)} %copy.91, bf16[6,1024,16,1]{1,2,0,3:T(8,128)(2,1)S(1)} %reshape.218, s32[6,4,1024]{2,0,1:T(8,128)S(1)} %copy.76), kind=kOutput, calls=%fused_computation.29.clone.1 | convolution fusion | flops 207618048 | bytes 393220 | tf_op jit(solution)/shard_map/while/body/eval_jaxpr/qfnb,qnk->bfk/dot_general | solution.py:96
  276.1 8.6 %fusion.33 = f32[24,256,4,16]{1,3,2,0:T(8,128)S(1)} fusion(f32[24,256,4,16]{1,3,2,0:T(8,128)S(1)} %get-tuple-element.361, s32[]{:T(128)S(6)} %copy.91, bf16[6,1024,16,1]{1,2,0,3:T(8,128)(2,1)S(1)} %reshape.218, s32[6,4,1024]{2,0,1:T(8,128)S(1)} %copy.76), kind=kOutput, calls=%fused_computation.29.clone.1 | convolution fusion | flops 207618048 | bytes 393220 | tf_op jit(solution)/shard_map/while/body/eval_jaxpr/qfnb,qnk->bfk/dot_general | solution.py:96
  288.7 8.6 %fusion.33 = f32[24,256,4,16]{1,3,2,0:T(8,128)S(1)} fusion(f32[24,256,4,16]{1,3,2,0:T(8,128)S(1)} %get-tuple-element.361, s32[]{:T(128)S(6)} %copy.91, bf16[6,1024,16,1]{1,2,0,3:T(8,128)(2,1)S(1)} %reshape.218, s32[6,4,1024]{2,0,1:T(8,128)S(1)} %copy.76), kind=kOutput, calls=%fused_computation.29.clone.1 | convolution fusion | flops 207618048 | bytes 393220 | tf_op jit(solution)/shard_map/while/body/eval_jaxpr/qfnb,qnk->bfk/dot_general | solution.py:96
  301.3 8.6 %fusion.33 = f32[24,256,4,16]{1,3,2,0:T(8,128)S(1)} fusion(f32[24,256,4,16]{1,3,2,0:T(8,128)S(1)} %get-tuple-element.361, s32[]{:T(128)S(6)} %copy.91, bf16[6,1024,16,1]{1,2,0,3:T(8,128)(2,1)S(1)} %reshape.218, s32[6,4,1024]{2,0,1:T(8,128)S(1)} %copy.76), kind=kOutput, calls=%fused_computation.29.clone.1 | convolution fusion | flops 207618048 | bytes 393220 | tf_op jit(solution)/shard_map/while/body/eval_jaxpr/qfnb,qnk->bfk/dot_general | solution.py:96
  313.9 8.6 %fusion.33 = f32[24,256,4,16]{1,3,2,0:T(8,128)S(1)} fusion(f32[24,256,4,16]{1,3,2,0:T(8,128)S(1)} %get-tuple-element.361, s32[]{:T(128)S(6)} %copy.91, bf16[6,1024,16,1]{1,2,0,3:T(8,128)(2,1)S(1)} %reshape.218, s32[6,4,1024]{2,0,1:T(8,128)S(1)} %copy.76), kind=kOutput, calls=%fused_computation.29.clone.1 | convolution fusion | flops 207618048 | bytes 393220 | tf_op jit(solution)/shard_map/while/body/eval_jaxpr/qfnb,qnk->bfk/dot_general | solution.py:96
  326.5 8.6 %fusion.33 = f32[24,256,4,16]{1,3,2,0:T(8,128)S(1)} fusion(f32[24,256,4,16]{1,3,2,0:T(8,128)S(1)} %get-tuple-element.361, s32[]{:T(128)S(6)} %copy.91, bf16[6,1024,16,1]{1,2,0,3:T(8,128)(2,1)S(1)} %reshape.218, s32[6,4,1024]{2,0,1:T(8,128)S(1)} %copy.76), kind=kOutput, calls=%fused_computation.29.clone.1 | convolution fusion | flops 207618048 | bytes 393220 | tf_op jit(solution)/shard_map/while/body/eval_jaxpr/qfnb,qnk->bfk/dot_general | solution.py:96
  339.1 8.6 %fusion.33 = f32[24,256,4,16]{1,3,2,0:T(8,128)S(1)} fusion(f32[24,256,4,16]{1,3,2,0:T(8,128)S(1)} %get-tuple-element.361, s32[]{:T(128)S(6)} %copy.91, bf16[6,1024,16,1]{1,2,0,3:T(8,128)(2,1)S(1)} %reshape.218, s32[6,4,1024]{2,0,1:T(8,128)S(1)} %copy.76), kind=kOutput, calls=%fused_computation.29.clone.1 | convolution fusion | flops 207618048 | bytes 393220 | tf_op jit(solution)/shard_map/while/body/eval_jaxpr/qfnb,qnk->bfk/dot_general | solution.py:96
  364.3 8.6 %fusion.33 = f32[24,256,4,16]{1,3,2,0:T(8,128)S(1)} fusion(f32[24,256,4,16]{1,3,2,0:T(8,128)S(1)} %get-tuple-element.361, s32[]{:T(128)S(6)} %copy.91, bf16[6,1024,16,1]{1,2,0,3:T(8,128)(2,1)S(1)} %reshape.218, s32[6,4,1024]{2,0,1:T(8,128)S(1)} %copy.76), kind=kOutput, calls=%fused_computation.29.clone.1 | convolution fusion | flops 207618048 | bytes 393220 | tf_op jit(solution)/shard_map/while/body/eval_jaxpr/qfnb,qnk->bfk/dot_general | solution.py:96
  376.9 8.6 %fusion.33 = f32[24,256,4,16]{1,3,2,0:T(8,128)S(1)} fusion(f32[24,256,4,16]{1,3,2,0:T(8,128)S(1)} %get-tuple-element.361, s32[]{:T(128)S(6)} %copy.91, bf16[6,1024,16,1]{1,2,0,3:T(8,128)(2,1)S(1)} %reshape.218, s32[6,4,1024]{2,0,1:T(8,128)S(1)} %copy.76), kind=kOutput, calls=%fused_computation.29.clone.1 | convolution fusion | flops 207618048 | bytes 393220 | tf_op jit(solution)/shard_map/while/body/eval_jaxpr/qfnb,qnk->bfk/dot_general | solution.py:96
  401.7 150.2 %all-reduce.2.cloned.1.call-done = f32[256,8,192]{0,1,2:T(8,128)} async-done(((f32[256,8,192]{0,1,2:T(8,128)}), f32[256,8,192]{0,1,2:T(8,128)}) %all-reduce.2.cloned.1.call-update) | async-done | bytes 1572880 | tf_op jit(solution)/shard_map/psum | solution.py:142
  560.0 18.0 %reduce-window.16 = f32[2,8,96,2,128]{4,2,3,1,0:T(8,128)S(1)} reduce-window(f32[2,8,96,2,128]{4,2,3,1,0:T(8,128)} %copy.56, f32[]{:T(128)} %constant.15.clone.1), window={size=1x1x1x1x128 pad=0_0x0_0x0_0x0_0x127_0}, to_apply=%region_13.14 | reduce-window | flops 49938432 | bytes 3145732 | tf_op jit(solution)/shard_map/reduce-window.2
  584.2 17.5 %pmax.7 = f32[8]{0:T(128)} all-reduce(f32[8]{0:T(128)S(1)} %subtract_reduce_fusion), channel_id=1, replica_groups=mesh['row'=32,'feat'=8] {'feat'}, use_global_device_ids=true, to_apply=%region_17.18 | all-reduce | flops 8 | bytes 64 | tf_op jit(solution)/shard_map/pmax | solution.py:147
  (262 shorter events, 179.6 us)
Async XLA Ops:
  7.2 544.8 %all-reduce.2.cloned.1.call-start = ((), (), s32[]{:S(2)}) async-start(), calls=%async_computation | async-start | bytes 3145728 | tf_op jit(solution)/shard_map/psum | solution.py:142
  22.8 72.8 %copy-start.3 = (s32[6,1024]{1,0:T(8,128)S(1)}, s32[6,1024]{1,0:T(8,128)}, u32[]{:S(2)}) copy-start(s32[6,1024]{1,0:T(8,128)} %param.15) | copy-start | bytes 73732
  399.0 1.3 copy-start.4
  399.0 1.5 copy-start.2
  551.9 2.1 copy-start
  579.6 2.6 copy-start.1
Sparse Core Ops, SparseCore 0:
  400.5 151.4 all-reduce.1
where the time goes:
time: 613 us; the launch traced here: 609 us
  matrix products  207 us (34%)
  waiting for transfers between devices  150 us (24%)
  other arithmetic  77.6 us (13%)
  local copies, waits for them, and re-layouts  76.8 us (13%)
  loops' own time  64.7 us (11%)
  blocking collectives  17.5 us (3%)
  between operations  14.3 us (2%)
    dot_general x24, matrix products, one_block(): jnp.einsum('qfnb,qnk->bfk', one_hot, weights, preferred_element_type=jnp....  207 us
    psum x1, waiting for transfers between devices, shards(): all_bins = lax.psum(bin_histogram(bin_codes, weights, bin_total), 'row')  150 us
    another operation x1, loops' own time, bin_histogram(): lax.map(one_block, jnp.arange(feat_dev // feat_block, dtype=jnp.int32) *...  47.8 us
    reduce_sum x8, other arithmetic, pair_block(): jnp.sum(jnp.where(live_pair, pair_prob * (1.0 - pair_prob) * pair_weight,...  35.9 us
    another operation x8, other arithmetic  28 us
    dynamic_slice x48, local copies, waits for them, and re-layouts, one_block(): code_block = lax.dynamic_slice_in_dim(bin_codes, first_feat, feat_block, 1)  26.2 us
    pmax x1, blocking collectives, shards(): best_gain = lax.pmax(jnp.max(gains, axis=(0, 2)), 'feat')  17.5 us
    another operation x1, loops' own time, shards(): lax.map(block_terms, jnp.arange(feat_count, dtype=jnp.int32) * row_span)  16.9 us
  transfers between devices with their start and end apart: 1, of which 1 were waited for; matrix products, arithmetic and copies ran while one was open for 0% of the time, Pallas kernels for 0%

commit v1 on v0

--- a/solution.py
+++ b/solution.py
@@ -139,7 +139,8 @@
     feat_dev = bin_codes.shape[1]
     bin_span = parent_hist.shape[0]
     bin_total = bin_span * lax.axis_size("row")
-    all_bins = lax.psum(bin_histogram(bin_codes, weights, bin_total), "row")
+    x_in = bin_histogram(bin_codes, weights, bin_total)
+    all_bins = lax.all_gather(x_in, "row").sum(axis=0)
     stacked_all = all_bins.reshape(bin_total, parents, feat_dev, 2)
     left_sums = jnp.cumsum(stacked_all, axis=0)
     totals = jnp.sum(stacked_all, axis=0)

time: 613 us -> 813 us (1.33)
  waiting for transfers between devices: 150 us -> 334 us
  other arithmetic: 77.6 us -> 96 us
    all_gather x0 -> x1, waiting for transfers between devices: none -> 334 us  [shards(): all_bins = lax.all_gather(x_in, 'row').sum(axis=0)]
    psum x1 -> x0, waiting for transfers between devices: 150 us -> none  [shards(): all_bins = lax.psum(bin_histogram(bin_codes, weights, bin_total), 'row')]
    reduce_sum x1, other arithmetic: 1.81 us -> 18.5 us  [shards(): totals = jnp.sum(stacked_all, axis=0)]
where the time goes in v1:
time: 813 us; the launch traced here: 808 us
  waiting for transfers between devices  334 us (41%)
  matrix products  207 us (25%)
  other arithmetic  96 us (12%)
  local copies, waits for them, and re-layouts  78.3 us (10%)
  loops' own time  64.7 us (8%)
  between operations  14.3 us (2%)
  blocking collectives  13.7 us (2%)
    all_gather x1, waiting for transfers between devices, shards(): all_bins = lax.all_gather(x_in, 'row').sum(axis=0)  334 us
    dot_general x24, matrix products, one_block(): jnp.einsum('qfnb,qnk->bfk', one_hot, weights, preferred_element_type=jnp....  207 us
    another operation x1, loops' own time, bin_histogram(): lax.map(one_block, jnp.arange(feat_dev // feat_block, dtype=jnp.int32) *...  47.8 us
    reduce_sum x8, other arithmetic, pair_block(): jnp.sum(jnp.where(live_pair, pair_prob * (1.0 - pair_prob) * pair_weight,...  35.7 us
    another operation x8, other arithmetic  29.1 us
    dynamic_slice x48, local copies, waits for them, and re-layouts, one_block(): code_block = lax.dynamic_slice_in_dim(bin_codes, first_feat, feat_block, 1)  26.2 us
    reduce_sum x1, other arithmetic, shards(): totals = jnp.sum(stacked_all, axis=0)  18.5 us
    another operation x1, loops' own time, shards(): lax.map(block_terms, jnp.arange(feat_count, dtype=jnp.int32) * row_span)  16.9 us
  transfers between devices with their start and end apart: 1, of which 1 were waited for; matrix products, arithmetic and copies ran while one was open for 0% of the time, Pallas kernels for 0%

profile of v1, /device:TPU:1, one launch (start us, length us, event | category | flops | bytes accessed | tf_op | source)
XLA Modules:
  0.0 808.3 jit_solution(15287721487431708716)
XLA Ops:
  22.2 72.6 %while.24 = (s32[]{:T(128)}, bf16[8,6,128]{2,1,0:T(8,128)(2,1)S(1)}, bf16[8,6,128]{2,1,0:T(8,128)(2,1)S(1)}, s32[8]{0:T(128)S(1)}, s32[6,1024]{1,0:T(8,128)}, /*...) while((s32[]{:T(128)}, ...), condition=%wide.region_9.10_spmd.clone, body=%wide.region_6.9_spmd.clone.sunk | while | flops 19135748 | bytes 1181147 | solution.py:128
  95.0 302.4 %while.25 = (s32[]{:T(128)}, f32[24,256,4,16]{1,3,2,0:T(8,128)S(1)}, s32[24]{0:T(128)S(1)}, s32[6,96,1024]{2,1,0:T(8,128)}, bf16[6,1024,2]{1,2,0:T(2,128)(2,1)S(...) while((s32[]{:T(128)}, f32[24,256,4,16]{1,3,2,0:T(8,128)S(1)}, ...), condition=%wide.region_11.12_spmd.clone, body=%wide.region_10.11_spmd.clone.sunk | while | flops 207716352 | bytes 1499283 | solution.py:98
  111.5 8.6 %fusion.34 = f32[24,256,4,16]{1,3,2,0:T(8,128)S(1)} fusion(f32[24,256,4,16]{1,3,2,0:T(8,128)S(1)} %get-tuple-element.379, s32[]{:T(128)} %get-tuple-element.378, bf16[6,1024,16,1]{1,2,0,3:T(8,128)(2,1)S(1)} %reshape.214, s32[6,4,1024]{2,0,1:T(8,128)S(1)} %copy.119), kind=kOutput, calls=%fused_computation.29.clone.1 | convolution fusion | flops 207618048 | bytes 393220 | tf_op jit(solution)/shard_map/while/body/eval_jaxpr/qfnb,qnk->bfk/dot_general | solution.py:96
  124.1 8.6 %fusion.34 = f32[24,256,4,16]{1,3,2,0:T(8,128)S(1)} fusion(f32[24,256,4,16]{1,3,2,0:T(8,128)S(1)} %get-tuple-element.379, s32[]{:T(128)} %get-tuple-element.378, bf16[6,1024,16,1]{1,2,0,3:T(8,128)(2,1)S(1)} %reshape.214, s32[6,4,1024]{2,0,1:T(8,128)S(1)} %copy.119), kind=kOutput, calls=%fused_computation.29.clone.1 | convolution fusion | flops 207618048 | bytes 393220 | tf_op jit(solution)/shard_map/while/body/eval_jaxpr/qfnb,qnk->bfk/dot_general | solution.py:96
  136.8 8.6 %fusion.34 = f32[24,256,4,16]{1,3,2,0:T(8,128)S(1)} fusion(f32[24,256,4,16]{1,3,2,0:T(8,128)S(1)} %get-tuple-element.379, s32[]{:T(128)} %get-tuple-element.378, bf16[6,1024,16,1]{1,2,0,3:T(8,128)(2,1)S(1)} %reshape.214, s32[6,4,1024]{2,0,1:T(8,128)S(1)} %copy.119), kind=kOutput, calls=%fused_computation.29.clone.1 | convolution fusion | flops 207618048 | bytes 393220 | tf_op jit(solution)/shard_map/while/body/eval_jaxpr/qfnb,qnk->bfk/dot_general | solution.py:96
  149.4 8.6 %fusion.34 = f32[24,256,4,16]{1,3,2,0:T(8,128)S(1)} fusion(f32[24,256,4,16]{1,3,2,0:T(8,128)S(1)} %get-tuple-element.379, s32[]{:T(128)} %get-tuple-element.378, bf16[6,1024,16,1]{1,2,0,3:T(8,128)(2,1)S(1)} %reshape.214, s32[6,4,1024]{2,0,1:T(8,128)S(1)} %copy.119), kind=kOutput, calls=%fused_computation.29.clone.1 | convolution fusion | flops 207618048 | bytes 393220 | tf_op jit(solution)/shard_map/while/body/eval_jaxpr/qfnb,qnk->bfk/dot_general | solution.py:96
  162.0 8.6 %fusion.34 = f32[24,256,4,16]{1,3,2,0:T(8,128)S(1)} fusion(f32[24,256,4,16]{1,3,2,0:T(8,128)S(1)} %get-tuple-element.379, s32[]{:T(128)} %get-tuple-element.378, bf16[6,1024,16,1]{1,2,0,3:T(8,128)(2,1)S(1)} %reshape.214, s32[6,4,1024]{2,0,1:T(8,128)S(1)} %copy.119), kind=kOutput, calls=%fused_computation.29.clone.1 | convolution fusion | flops 207618048 | bytes 393220 | tf_op jit(solution)/shard_map/while/body/eval_jaxpr/qfnb,qnk->bfk/dot_general | solution.py:96
  174.6 8.6 %fusion.34 = f32[24,256,4,16]{1,3,2,0:T(8,128)S(1)} fusion(f32[24,256,4,16]{1,3,2,0:T(8,128)S(1)} %get-tuple-element.379, s32[]{:T(128)} %get-tuple-element.378, bf16[6,1024,16,1]{1,2,0,3:T(8,128)(2,1)S(1)} %reshape.214, s32[6,4,1024]{2,0,1:T(8,128)S(1)} %copy.119), kind=kOutput, calls=%fused_computation.29.clone.1 | convolution fusion | flops 207618048 | bytes 393220 | tf_op jit(solution)/shard_map/while/body/eval_jaxpr/qfnb,qnk->bfk/dot_general | solution.py:96
  187.2 8.6 %fusion.34 = f32[24,256,4,16]{1,3,2,0:T(8,128)S(1)} fusion(f32[24,256,4,16]{1,3,2,0:T(8,128)S(1)} %get-tuple-element.379, s32[]{:T(128)} %get-tuple-element.378, bf16[6,1024,16,1]{1,2,0,3:T(8,128)(2,1)S(1)} %reshape.214, s32[6,4,1024]{2,0,1:T(8,128)S(1)} %copy.119), kind=kOutput, calls=%fused_computation.29.clone.1 | convolution fusion | flops 207618048 | bytes 393220 | tf_op jit(solution)/shard_map/while/body/eval_jaxpr/qfnb,qnk->bfk/dot_general | solution.py:96
  199.8 8.6 %fusion.34 = f32[24,256,4,16]{1,3,2,0:T(8,128)S(1)} fusion(f32[24,256,4,16]{1,3,2,0:T(8,128)S(1)} %get-tuple-element.379, s32[]{:T(128)} %get-tuple-element.378, bf16[6,1024,16,1]{1,2,0,3:T(8,128)(2,1)S(1)} %reshape.214, s32[6,4,1024]{2,0,1:T(8,128)S(1)} %copy.119), kind=kOutput, calls=%fused_computation.29.clone.1 | convolution fusion | flops 207618048 | bytes 393220 | tf_op jit(solution)/shard_map/while/body/eval_jaxpr/qfnb,qnk->bfk/dot_general | solution.py:96
  212.4 8.6 %fusion.34 = f32[24,256,4,16]{1,3,2,0:T(8,128)S(1)} fusion(f32[24,256,4,16]{1,3,2,0:T(8,128)S(1)} %get-tuple-element.379, s32[]{:T(128)} %get-tuple-element.378, bf16[6,1024,16,1]{1,2,0,3:T(8,128)(2,1)S(1)} %reshape.214, s32[6,4,1024]{2,0,1:T(8,128)S(1)} %copy.119), kind=kOutput, calls=%fused_computation.29.clone.1 | convolution fusion | flops 207618048 | bytes 393220 | tf_op jit(solution)/shard_map/while/body/eval_jaxpr/qfnb,qnk->bfk/dot_general | solution.py:96
  225.0 8.6 %fusion.34 = f32[24,256,4,16]{1,3,2,0:T(8,128)S(1)} fusion(f32[24,256,4,16]{1,3,2,0:T(8,128)S(1)} %get-tuple-element.379, s32[]{:T(128)} %get-tuple-element.378, bf16[6,1024,16,1]{1,2,0,3:T(8,128)(2,1)S(1)} %reshape.214, s32[6,4,1024]{2,0,1:T(8,128)S(1)} %copy.119), kind=kOutput, calls=%fused_computation.29.clone.1 | convolution fusion | flops 207618048 | bytes 393220 | tf_op jit(solution)/shard_map/while/body/eval_jaxpr/qfnb,qnk->bfk/dot_general | solution.py:96
  237.6 8.6 %fusion.34 = f32[24,256,4,16]{1,3,2,0:T(8,128)S(1)} fusion(f32[24,256,4,16]{1,3,2,0:T(8,128)S(1)} %get-tuple-element.379, s32[]{:T(128)} %get-tuple-element.378, bf16[6,1024,16,1]{1,2,0,3:T(8,128)(2,1)S(1)} %reshape.214, s32[6,4,1024]{2,0,1:T(8,128)S(1)} %copy.119), kind=kOutput, calls=%fused_computation.29.clone.1 | convolution fusion | flops 207618048 | bytes 393220 | tf_op jit(solution)/shard_map/while/body/eval_jaxpr/qfnb,qnk->bfk/dot_general | solution.py:96
  250.2 8.6 %fusion.34 = f32[24,256,4,16]{1,3,2,0:T(8,128)S(1)} fusion(f32[24,256,4,16]{1,3,2,0:T(8,128)S(1)} %get-tuple-element.379, s32[]{:T(128)} %get-tuple-element.378, bf16[6,1024,16,1]{1,2,0,3:T(8,128)(2,1)S(1)} %reshape.214, s32[6,4,1024]{2,0,1:T(8,128)S(1)} %copy.119), kind=kOutput, calls=%fused_computation.29.clone.1 | convolution fusion | flops 207618048 | bytes 393220 | tf_op jit(solution)/shard_map/while/body/eval_jaxpr/qfnb,qnk->bfk/dot_general | solution.py:96
  262.8 8.6 %fusion.34 = f32[24,256,4,16]{1,3,2,0:T(8,128)S(1)} fusion(f32[24,256,4,16]{1,3,2,0:T(8,128)S(1)} %get-tuple-element.379, s32[]{:T(128)} %get-tuple-element.378, bf16[6,1024,16,1]{1,2,0,3:T(8,128)(2,1)S(1)} %reshape.214, s32[6,4,1024]{2,0,1:T(8,128)S(1)} %copy.119), kind=kOutput, calls=%fused_computation.29.clone.1 | convolution fusion | flops 207618048 | bytes 393220 | tf_op jit(solution)/shard_map/while/body/eval_jaxpr/qfnb,qnk->bfk/dot_general | solution.py:96
  275.4 8.6 %fusion.34 = f32[24,256,4,16]{1,3,2,0:T(8,128)S(1)} fusion(f32[24,256,4,16]{1,3,2,0:T(8,128)S(1)} %get-tuple-element.379, s32[]{:T(128)} %get-tuple-element.378, bf16[6,1024,16,1]{1,2,0,3:T(8,128)(2,1)S(1)} %reshape.214, s32[6,4,1024]{2,0,1:T(8,128)S(1)} %copy.119), kind=kOutput, calls=%fused_computation.29.clone.1 | convolution fusion | flops 207618048 | bytes 393220 | tf_op jit(solution)/shard_map/while/body/eval_jaxpr/qfnb,qnk->bfk/dot_general | solution.py:96
  300.6 8.6 %fusion.34 = f32[24,256,4,16]{1,3,2,0:T(8,128)S(1)} fusion(f32[24,256,4,16]{1,3,2,0:T(8,128)S(1)} %get-tuple-element.379, s32[]{:T(128)} %get-tuple-element.378, bf16[6,1024,16,1]{1,2,0,3:T(8,128)(2,1)S(1)} %reshape.214, s32[6,4,1024]{2,0,1:T(8,128)S(1)} %copy.119), kind=kOutput, calls=%fused_computation.29.clone.1 | convolution fusion | flops 207618048 | bytes 393220 | tf_op jit(solution)/shard_map/while/body/eval_jaxpr/qfnb,qnk->bfk/dot_general | solution.py:96
  325.8 8.6 %fusion.34 = f32[24,256,4,16]{1,3,2,0:T(8,128)S(1)} fusion(f32[24,256,4,16]{1,3,2,0:T(8,128)S(1)} %get-tuple-element.379, s32[]{:T(128)} %get-tuple-element.378, bf16[6,1024,16,1]{1,2,0,3:T(8,128)(2,1)S(1)} %reshape.214, s32[6,4,1024]{2,0,1:T(8,128)S(1)} %copy.119), kind=kOutput, calls=%fused_computation.29.clone.1 | convolution fusion | flops 207618048 | bytes 393220 | tf_op jit(solution)/shard_map/while/body/eval_jaxpr/qfnb,qnk->bfk/dot_general | solution.py:96
  351.1 8.6 %fusion.34 = f32[24,256,4,16]{1,3,2,0:T(8,128)S(1)} fusion(f32[24,256,4,16]{1,3,2,0:T(8,128)S(1)} %get-tuple-element.379, s32[]{:T(128)} %get-tuple-element.378, bf16[6,1024,16,1]{1,2,0,3:T(8,128)(2,1)S(1)} %reshape.214, s32[6,4,1024]{2,0,1:T(8,128)S(1)} %copy.119), kind=kOutput, calls=%fused_computation.29.clone.1 | convolution fusion | flops 207618048 | bytes 393220 | tf_op jit(solution)/shard_map/while/body/eval_jaxpr/qfnb,qnk->bfk/dot_general | solution.py:96
  363.7 8.6 %fusion.34 = f32[24,256,4,16]{1,3,2,0:T(8,128)S(1)} fusion(f32[24,256,4,16]{1,3,2,0:T(8,128)S(1)} %get-tuple-element.379, s32[]{:T(128)} %get-tuple-element.378, bf16[6,1024,16,1]{1,2,0,3:T(8,128)(2,1)S(1)} %reshape.214, s32[6,4,1024]{2,0,1:T(8,128)S(1)} %copy.119), kind=kOutput, calls=%fused_computation.29.clone.1 | convolution fusion | flops 207618048 | bytes 393220 | tf_op jit(solution)/shard_map/while/body/eval_jaxpr/qfnb,qnk->bfk/dot_general | solution.py:96
  401.5 333.8 %all-gather.2.cloned.1.call-done = f32[32,256,8,192]{1,3,2,0:T(8,128)} async-done(((f32[1,256,8,192]{1,3,2,0:T(8,128)}), f32[32,256,8,192]{1,3,2,0:T(8,128)}) %all-gather.2.cloned.1.call-update) | async-done | bytes 50331664 | tf_op jit(solution)/shard_map/all_gather | solution.py:143
  735.3 18.5 %fusion.26 = (f32[8,192]{1,0:T(8,128)S(1)}, f32[256,8,192]{0,2,1:T(8,128)S(1)}) fusion(f32[32,256,8,192]{1,3,2,0:T(8,128)} %all-gather.2.cloned.1.call-done), kind=kLoop, calls=%fused_computation.70 | loop fusion | flops 24771072 | bytes 51910656 | tf_op jit(solution)/shard_map/reduce_sum | solution.py:146
  760.3 18.0 %reduce-window.16 = f32[2,8,96,2,128]{4,2,3,1,0:T(8,128)S(1)} reduce-window(f32[2,8,96,2,128]{4,2,3,1,0:T(8,128)} %copy.98, f32[]{:T(128)} %constant.15.clone.1), window={size=1x1x1x1x128 pad=0_0x0_0x0_0x0_0x127_0}, to_apply=%region_13.14 | reduce-window | flops 49938432 | bytes 3145732 | tf_op jit(solution)/shard_map/reduce-window.2
  785.6 13.7 %pmax.7 = f32[8]{0:T(128)} all-reduce(f32[8]{0:T(128)S(1)} %subtract_reduce_fusion), channel_id=1, replica_groups=mesh['row'=32,'feat'=8] {'feat'}, use_global_device_ids=true, to_apply=%region_17.18 | all-reduce | flops 8 | bytes 64 | tf_op jit(solution)/shard_map/pmax | solution.py:148
  (263 shorter events, 189.8 us)
Async XLA Ops:
  7.2 728.1 %all-gather.2.cloned.1.call-start = ((), (), s32[]{:S(2)}) async-start(), calls=%async_computation | async-start | bytes 51904512 | tf_op jit(solution)/shard_map/all_gather | solution.py:143
  22.1 72.7 %copy-start.3 = (s32[8]{0:T(128)S(1)}, s32[8]{0:T(128)}, u32[]{:S(2)}) copy-start(s32[8]{0:T(128)} %param.16) | copy-start | bytes 100
  22.1 72.7 %copy-start.2 = (s32[6,1024]{1,0:T(8,128)S(1)}, s32[6,1024]{1,0:T(8,128)}, u32[]{:S(2)}) copy-start(s32[6,1024]{1,0:T(8,128)} %param.15) | copy-start | bytes 73732
  398.5 1.7 copy-start.1
  783.6 16.4 %copy-start = (f32[8,8,192]{1,0,2:T(8,128)S(1)}, f32[8,8,192]{1,0,2:T(8,128)}, u32[]{:S(2)}) copy-start(f32[8,8,192]{1,0,2:T(8,128)} %copy.95) | copy-start | bytes 147460
Sparse Core Ops, SparseCore 0:
  400.2 335.0 all-gather.1
